TPU v7x, 128 devices: a whole 4x4x4 slice. The times are simulated.
128 devices in a mesh: item: 4 (over z), user: 32 (over y, x, core).
Axes of the slice: x: 4, y: 4, z: 4, core: 2. Of those that a mesh axis runs over, the one named last changes fastest.
Arguments:
- interactions: bfloat16 [65536, 16384], P('user', 'item'), may hold values from 0 to 1, as said below
- omega: float32 [16384, 256], P('item'), may hold values from -6 to 6
Outputs:
- scaled_basis: float32 [16384, 256], P('item')
Inputs may be any that keep to these rules, and one draw needn't show every extreme that they name: `interactions`: every entry is 0 or 1.
All inputs are finite; a program needn't handle non-finite values.
Results may differ from a plain program's by a relative error of at most 0.0003.
Values sent between devices are 32-bit elements; how exact they have to be, the bound alone decides.
No kernel may reach another device: no remote copies, remote signals or barrier semaphores. Data moves between devices by JAX's collectives and lax.ppermute only.
A program may use at most 128 MiB of HBM per device.

v0:
```python
import jax
import jax.numpy as jnp
from jax import lax
from jax.sharding import PartitionSpec as P

ridge = 200.0
highest = lax.Precision.HIGHEST


def gram_of(block):
    return lax.dot_general(
        block,
        block,
        (((0,), (0,)), ((), ())),
        precision=highest,
        preferred_element_type=jnp.float32,
    )


def factor(block, gram):
    lower = jnp.linalg.cholesky(gram)
    return lax.linalg.triangular_solve(lower, block, left_side=False, lower=True, transpose_a=True)


def gram_wide(block):
    return lax.psum(gram_of(block), ("item", "user"))


def local(interactions, omega):
    local_rows = jnp.dot(interactions, omega, precision=highest, preferred_element_type=jnp.float32)
    user_sketch = lax.psum(local_rows, "item")
    item_count = omega.shape[0] * lax.axis_size("item")
    factor_scale = jnp.sqrt(jnp.float32(item_count))
    own_rows = omega.shape[0] // lax.axis_size("user")
    block = lax.psum_scatter(
        lax.dot_general(
            interactions,
            user_sketch,
            (((0,), (0,)), ((), ())),
            precision=highest,
            preferred_element_type=jnp.float32,
        ),
        "user",
        scatter_dimension=0,
        tiled=True,
    )
    own_omega = lax.dynamic_slice_in_dim(omega, lax.axis_index("user") * own_rows, own_rows, 0)
    block = block + ridge * own_omega
    for sweep in range(2):
        block = factor(block, gram_wide(block))
    return lax.all_gather(factor_scale * block, "user", axis=0, tiled=True)


def solution(mesh):
    in_specs = (P("user", "item"), P("item", None))
    out_specs = P("item", None)
    return jax.shard_map(local, mesh=mesh, in_specs=in_specs, out_specs=out_specs, check_vma=False)
```

profile of v0, /device:TPU:1, one launch (start us, length us, event | category | flops | bytes accessed | tf_op | source)
XLA Modules:
  0.0 661.8 jit_solution(2004291830693291663)
XLA Ops:
  6.5 0.0 all-reduce.5.cloned.1.call-start
  6.5 18.5 %fusion.27 = f32[2048,256]{1,0:T(8,128)} fusion(bf16[2048,4096]{1,0:T(8,128)(2,1)} %param.5, f32[4096,256]{1,0:T(8,128)} %param.6), kind=kOutput, calls=%fused_computation.63 | convolution fusion | flops 25769803776 | bytes 23068672 | tf_op jit(solution)/shard_map/dot_general | solution.py:30
  25.1 0.0 all-reduce.5.cloned.1.call-update
  25.1 0.0 reduce-scatter.2.cloned.1.call-start
  25.1 62.1 %all-reduce.5.cloned.1.call-done = f32[2048,256]{1,0:T(8,128)} async-done(((f32[2048,256]{1,0:T(8,128)}), f32[2048,256]{1,0:T(8,128)}) %all-reduce.5.cloned.1.call-update) | async-done | bytes 2097168 | tf_op jit(solution)/shard_map/psum | solution.py:31
  87.2 17.8 %convolution_bitcast_fusion = f32[4096,256]{0,1:T(8,128)} fusion(f32[2048,256]{1,0:T(8,128)} %all-reduce.5.cloned.1.call-done, bf16[2048,4096]{1,0:T(8,128)(2,1)} %param.5), kind=kOutput, calls=%fused_computation.4 | convolution fusion | flops 25769803776 | bytes 23068672 | tf_op jit(solution)/shard_map/dot_general | solution.py:36
  105.0 0.0 reduce-scatter.2.cloned.1.call-update
  105.0 0.0 all-reduce.7.cloned.1.call-start
  105.0 0.9 constant_dynamic-slice_fusion.2
  106.0 0.1 copy.11
  106.1 79.4 %reduce-scatter.2.cloned.1.call-done = f32[128,256]{0,1:T(8,128)} async-done(((f32[4096,256]{0,1:T(8,128)}), f32[128,256]{0,1:T(8,128)}) %reduce-scatter.2.cloned.1.call-update) | async-done | bytes 131088 | tf_op jit(solution)/shard_map/reduce_scatter | solution.py:35
  185.5 0.9 multiply_add_fusion
  186.4 1.1 fusion.28
  187.5 0.0 all-reduce.7.cloned.1.call-update
  187.5 0.2 all-reduce.9.cloned.1.call-start
  187.8 146.7 %all-reduce.7.cloned.1.call-done = f32[256,256]{0,1:T(8,128)} async-done(((f32[256,256]{0,1:T(8,128)}), f32[256,256]{0,1:T(8,128)}) %all-reduce.7.cloned.1.call-update) | async-done | bytes 262160 | tf_op jit(solution)/shard_map/psum | solution.py:26
  334.5 1.1 copy.5
  335.6 1.0 fusion.1
  336.6 11.7 %cholesky.130 = f32[128,128]{1,0:T(8,128)S(1)} custom-call(f32[128,128]{1,0:T(8,128)S(1)} %cholesky.194), custom_call_target="Cholesky" | custom-call | tf_op jit(solution)/shard_map/jit(cholesky)/cholesky | solution.py:21
  348.3 9.8 %custom-call.13 = f32[1,128,128]{1,2,0:T(8,128)S(1)} custom-call(f32[1,128,128]{2,1,0:T(8,128)S(1)} %get-tuple-element.50), custom_call_target="InvertDiagBlocksLowerTriangular" | custom-call | tf_op jit(solution)/shard_map/jit(cholesky)/cholesky | solution.py:21
  358.2 0.2 constant_dynamic-update-slice_fusion.3
  358.4 0.3 convolution_subtract_fusion.3
  358.6 11.7 %cholesky.147 = f32[128,128]{1,0:T(8,128)S(1)} custom-call(f32[128,128]{1,0:T(8,128)S(1)} %convolution_subtract_fusion.3), custom_call_target="Cholesky" | custom-call | tf_op jit(solution)/shard_map/jit(cholesky)/cholesky | solution.py:21
  370.4 0.7 compare_reduce_fusion.2
  372.5 0.1 broadcast.89
  372.6 4.1 while.4
  372.6 0.6 fusion.45
  373.2 1.4 bitcast_dynamic-update-slice_fusion.4
  374.7 0.6 fusion.45
  375.3 1.4 bitcast_dynamic-update-slice_fusion.4
  376.7 19.7 %custom-call.14 = f32[2,128,128]{1,2,0:T(8,128)S(1)} custom-call(f32[2,128,128]{2,1,0:T(8,128)S(1)} %get-tuple-element.21), custom_call_target="InvertDiagBlocksLowerTriangular" | custom-call | tf_op jit(solution)/shard_map/triangular_solve/custom-call.0 | solution.py:22
  396.4 0.3 fusion.13
  396.7 0.2 convolution_subtract_fusion.2
  396.9 0.3 fusion.11
  397.2 1.1 fusion.2
  398.3 0.0 all-reduce.9.cloned.1.call-update
  398.3 0.3 all-gather.2.cloned.1.call-start
  398.6 140.5 %all-reduce.9.cloned.1.call-done = f32[256,256]{0,1:T(8,128)} async-done(((f32[256,256]{0,1:T(8,128)}), f32[256,256]{0,1:T(8,128)}) %all-reduce.9.cloned.1.call-update) | async-done | bytes 262160 | tf_op jit(solution)/shard_map/psum | solution.py:26
  539.0 1.1 copy.7
  540.1 1.0 fusion
  541.1 11.7 %cholesky.164 = f32[128,128]{1,0:T(8,128)S(1)} custom-call(f32[128,128]{1,0:T(8,128)S(1)} %cholesky.197), custom_call_target="Cholesky" | custom-call | tf_op jit(solution)/shard_map/jit(cholesky)/cholesky | solution.py:21
  552.9 0.6 compare_reduce_fusion.1
  553.5 9.8 %custom-call.15 = f32[1,128,128]{1,2,0:T(8,128)S(1)} custom-call(f32[1,128,128]{2,1,0:T(8,128)S(1)} %get-tuple-element.46), custom_call_target="InvertDiagBlocksLowerTriangular" | custom-call | tf_op jit(solution)/shard_map/jit(cholesky)/cholesky | solution.py:21
  563.4 0.2 constant_dynamic-update-slice_fusion.1
  563.6 0.3 convolution_subtract_fusion.1
  563.8 11.7 %cholesky.181 = f32[128,128]{1,0:T(8,128)S(1)} custom-call(f32[128,128]{1,0:T(8,128)S(1)} %convolution_subtract_fusion.1), custom_call_target="Cholesky" | custom-call | tf_op jit(solution)/shard_map/jit(cholesky)/cholesky | solution.py:21
  575.6 0.7 compare_reduce_fusion
  577.7 4.4 while.5
  578.0 0.6 fusion.46
  578.6 1.4 bitcast_dynamic-update-slice_fusion.5
  580.0 0.6 fusion.46
  580.6 1.4 bitcast_dynamic-update-slice_fusion.5
  582.1 19.7 %custom-call.16 = f32[2,128,128]{1,2,0:T(8,128)S(1)} custom-call(f32[2,128,128]{2,1,0:T(8,128)S(1)} %get-tuple-element.22), custom_call_target="InvertDiagBlocksLowerTriangular" | custom-call | tf_op jit(solution)/shard_map/triangular_solve/custom-call.0 | solution.py:22
  601.8 0.3 fusion.8
  602.1 0.2 convolution_subtract_fusion
  602.3 0.3 fusion.6
  602.6 0.7 maximum_multiply_fusion
  603.2 0.0 all-gather.2.cloned.1.call-update
  603.3 46.4 %all-gather.2.cloned.1.call-done = f32[4096,256]{0,1:T(8,128)} async-done(((f32[128,256]{0,1:T(8,128)}), f32[4096,256]{0,1:T(8,128)}) %all-gather.2.cloned.1.call-update) | async-done | bytes 4194320 | tf_op jit(solution)/shard_map/all_gather | solution.py:51
  649.7 5.6 copy.8
  (17 shorter events, 0.3 us)
Async XLA Ops:
  6.5 80.7 %all-reduce.5.cloned.1.call-start = ((), (), s32[]{:S(2)}) async-start(), calls=%async_computation.1 | async-start | bytes 4194304 | tf_op jit(solution)/shard_map/psum | solution.py:31
  25.1 160.4 %reduce-scatter.2.cloned.1.call-start = ((), (), s32[]{:S(2)}) async-start(), calls=%async_computation.2 | async-start | bytes 4325376 | tf_op jit(solution)/shard_map/reduce_scatter | solution.py:35
  105.0 229.5 %all-reduce.7.cloned.1.call-start = ((), (), s32[]{:S(2)}) async-start(), calls=%async_computation.3 | async-start | bytes 524288 | tf_op jit(solution)/shard_map/psum | solution.py:26
  187.5 351.5 %all-reduce.9.cloned.1.call-start = ((), (), s32[]{:S(2)}) async-start(), calls=%async_computation.4 | async-start | bytes 524288 | tf_op jit(solution)/shard_map/psum | solution.py:26
  398.3 251.4 %all-gather.2.cloned.1.call-start = ((), (), s32[]{:S(2)}) async-start(), calls=%async_computation.5 | async-start | bytes 4325376 | tf_op jit(solution)/shard_map/all_gather | solution.py:51
Sparse Core Ops, SparseCore 0:
  25.2 61.9 all-reduce.4
  105.1 80.3 reduce-scatter.1
  190.3 144.1 all-reduce.6
  398.4 140.5 all-reduce.8
  603.4 46.2 all-gather.1
where the time goes:
time: 662 us
  waiting for transfers between devices  475 us (72%)
  other arithmetic  112 us (17%)
  matrix products  40.9 us (6%)
  local copies, waits for them, and re-layouts  17 us (3%)
  between operations  16 us (2%)
    psum x2, waiting for transfers between devices, gram_wide(): return lax.psum(gram_of(block), ('item', 'user'))  287 us
    reduce_scatter x1, waiting for transfers between devices, local(): lax.psum_scatter(lax.dot_general(interactions, user_sketch, (((0,), (0,))...  79.4 us
    another operation x13, other arithmetic, factor(): lower = jnp.linalg.cholesky(gram)  68.7 us
    psum x1, waiting for transfers between devices, local(): user_sketch = lax.psum(local_rows, 'item')  62.1 us
    all_gather x1, waiting for transfers between devices, local(): return lax.all_gather(factor_scale * block, 'user', axis=0, tiled=True)  46.4 us
    another operation x5, other arithmetic, factor(): lax.linalg.triangular_solve(lower, block, left_side=False, lower=True, tr...  39.4 us
    dot_general x1, matrix products, local(): jnp.dot(interactions, omega, precision=highest, preferred_element_type=jn...  18.5 us
    dot_general x1, matrix products, local(): lax.dot_general(interactions, user_sketch, (((0,), (0,)), ((), ())), prec...  17.8 us
  transfers between devices with their start and end apart: 5, of which 5 were waited for; matrix products, arithmetic and copies ran while one was open for 0% of the time, Pallas kernels for 0%

commit v1 on v0

--- a/solution.py
+++ b/solution.py
@@ -1,10 +1,24 @@
+import functools
 import jax
 import jax.numpy as jnp
 from jax import lax
 from jax.sharding import PartitionSpec as P
+from jax.lax import axis_size, ppermute
 
 ridge = 200.0
 highest = lax.Precision.HIGHEST
+
+
+def spread_the_zones(field, mesh_name):
+    devs = axis_size(mesh_name)
+    known = field
+    ready = lambda taken_in: [(ix, ix ^ taken_in) for ix in range(devs)]
+    for c in range(devs.bit_length() - 1):
+        known = known + ppermute(known, mesh_name, ready(1 << c))
+    return known
+
+
+rounds_pack = functools.partial(spread_the_zones, mesh_name="item")
 
 
 def gram_of(block):
@@ -28,7 +42,7 @@
 
 def local(interactions, omega):
     local_rows = jnp.dot(interactions, omega, precision=highest, preferred_element_type=jnp.float32)
-    user_sketch = lax.psum(local_rows, "item")
+    user_sketch = rounds_pack(local_rows)
     item_count = omega.shape[0] * lax.axis_size("item")
     factor_scale = jnp.sqrt(jnp.float32(item_count))
     own_rows = omega.shape[0] // lax.axis_size("user")

time: 662 us -> 704 us (1.063); the launches traced: 662 us -> 695 us
  waiting for transfers between devices: 475 us -> 506 us
    ppermute x0 -> x2, waiting for transfers between devices: none -> 89.8 us  [spread_the_zones(): known = known + ppermute(known, mesh_name, ready(1 << c))]
    psum x1 -> x0, waiting for transfers between devices: 62.1 us -> none  [local(): user_sketch = lax.psum(local_rows, 'item')]
  transfers between devices with their start and end apart: 5 -> 6, of which waited for: 5 -> 6; matrix products, arithmetic and copies ran while one was open for 0% -> 0% of each run, Pallas kernels for 0% -> 0%
where the time goes in v1:
time: 704 us; the launch traced here: 695 us
  waiting for transfers between devices  506 us (72%)
  other arithmetic  112 us (16%)
  matrix products  37.2 us (5%)
  local copies, waits for them, and re-layouts  17 us (2%)
  between operations  16.3 us (2%)
    psum x2, waiting for transfers between devices, gram_wide(): return lax.psum(gram_of(block), ('item', 'user'))  287 us
    ppermute x2, waiting for transfers between devices, spread_the_zones(): known = known + ppermute(known, mesh_name, ready(1 << c))  89.8 us
    reduce_scatter x1, waiting for transfers between devices, local(): lax.psum_scatter(lax.dot_general(interactions, user_sketch, (((0,), (0,))...  82.8 us
    another operation x13, other arithmetic, factor(): lower = jnp.linalg.cholesky(gram)  68.7 us
    all_gather x1, waiting for transfers between devices, local(): return lax.all_gather(factor_scale * block, 'user', axis=0, tiled=True)  46.4 us
    another operation x5, other arithmetic, factor(): lax.linalg.triangular_solve(lower, block, left_side=False, lower=True, tr...  39.4 us
    dot_general x1, matrix products, local(): jnp.dot(interactions, omega, precision=highest, preferred_element_type=jn...  17.5 us
    dot_general x1, matrix products, local(): lax.dot_general(interactions, user_sketch, (((0,), (0,)), ((), ())), prec...  15 us
  transfers between devices with their start and end apart: 6, of which 6 were waited for; matrix products, arithmetic and copies ran while one was open for 0% of the time, Pallas kernels for 0%

profile of v1, /device:TPU:1, one launch (start us, length us, event | category | flops | bytes accessed | tf_op | source)
XLA Modules:
  0.0 695.4 jit_solution(16740009601428446785)
XLA Ops:
  6.5 0.0 reduce-scatter.2.cloned.1.call-start
  6.5 0.0 copy-start
  6.5 17.5 %fusion.29 = f32[2048,256]{1,0:T(8,128)S(1)} fusion(bf16[2048,4096]{1,0:T(8,128)(2,1)} %param.5, f32[4096,256]{1,0:T(8,128)} %param.6), kind=kOutput, calls=%fused_computation.65 | convolution fusion | flops 25769803776 | bytes 23068672 | tf_op jit(solution)/shard_map/dot_general | solution.py:44
  24.1 2.5 collective-permute-start
  26.6 45.3 %collective-permute-done = f32[2048,256]{1,0:T(8,128)S(1)} collective-permute-done((f32[2048,256]{1,0:T(8,128)S(1)}, f32[2048,256]{1,0:T(8,128)S(1)}, u32[]{:S(2)}, u32[]{:S(2)}) %collective-permute-start) | collective-permute-done | bytes 2097184 | tf_op jit(solution)/shard_map/ppermute | solution.py:17
  72.0 0.3 add.35
  72.2 3.2 collective-permute-start.1
  75.4 44.5 %collective-permute-done.1 = f32[2048,256]{1,0:T(8,128)S(1)} collective-permute-done((f32[2048,256]{1,0:T(8,128)S(1)}, f32[2048,256]{1,0:T(8,128)S(1)}, u32[]{:S(2)}, u32[]{:S(2)}) %collective-permute-start.1) | collective-permute-done | bytes 2097184 | tf_op jit(solution)/shard_map/ppermute | solution.py:17
  119.9 0.0 copy-done
  119.9 15.0 %convolution_bitcast_fusion = f32[4096,256]{0,1:T(8,128)} fusion(bf16[2048,4096]{1,0:T(8,128)(2,1)S(1)} %copy-done, f32[2048,256]{1,0:T(8,128)S(1)} %add.35, f32[2048,256]{1,0:T(8,128)S(1)} %collective-permute-done.1), kind=kOutput, calls=%fused_computation.4 | convolution fusion | flops 25770328064 | bytes 25165824 | tf_op jit(solution)/shard_map/dot_general | solution.py:50
  134.9 0.0 reduce-scatter.2.cloned.1.call-update
  134.9 0.0 all-reduce.4.cloned.1.call-start
  135.0 0.9 constant_dynamic-slice_fusion.2
  135.9 0.1 copy.11
  136.0 82.8 %reduce-scatter.2.cloned.1.call-done = f32[128,256]{0,1:T(8,128)} async-done(((f32[4096,256]{0,1:T(8,128)}), f32[128,256]{0,1:T(8,128)}) %reduce-scatter.2.cloned.1.call-update) | async-done | bytes 131088 | tf_op jit(solution)/shard_map/reduce_scatter | solution.py:49
  218.8 0.9 multiply_add_fusion
  219.8 1.1 fusion.30
  220.8 0.0 all-reduce.4.cloned.1.call-update
  220.9 0.5 all-reduce.6.cloned.1.call-start
  221.4 146.5 %all-reduce.4.cloned.1.call-done = f32[256,256]{0,1:T(8,128)} async-done(((f32[256,256]{0,1:T(8,128)}), f32[256,256]{0,1:T(8,128)}) %all-reduce.4.cloned.1.call-update) | async-done | bytes 262160 | tf_op jit(solution)/shard_map/psum | solution.py:40
  367.9 1.1 copy.5
  369.0 1.0 fusion.2
  370.0 11.7 %cholesky.130 = f32[128,128]{1,0:T(8,128)S(1)} custom-call(f32[128,128]{1,0:T(8,128)S(1)} %cholesky.194), custom_call_target="Cholesky" | custom-call | tf_op jit(solution)/shard_map/jit(cholesky)/cholesky | solution.py:35
  381.8 9.8 %custom-call.13 = f32[1,128,128]{1,2,0:T(8,128)S(1)} custom-call(f32[1,128,128]{2,1,0:T(8,128)S(1)} %get-tuple-element.50), custom_call_target="InvertDiagBlocksLowerTriangular" | custom-call | tf_op jit(solution)/shard_map/jit(cholesky)/cholesky | solution.py:35
  391.6 0.2 constant_dynamic-update-slice_fusion.3
  391.8 0.3 convolution_subtract_fusion.2
  392.1 11.7 %cholesky.147 = f32[128,128]{1,0:T(8,128)S(1)} custom-call(f32[128,128]{1,0:T(8,128)S(1)} %convolution_subtract_fusion.2), custom_call_target="Cholesky" | custom-call | tf_op jit(solution)/shard_map/jit(cholesky)/cholesky | solution.py:35
  403.8 0.7 compare_reduce_fusion.2
  405.9 0.1 broadcast.89
  406.0 4.1 while.4
  406.0 0.6 fusion.45
  406.6 1.4 bitcast_dynamic-update-slice_fusion.4
  408.1 0.6 fusion.45
  408.7 1.4 bitcast_dynamic-update-slice_fusion.4
  410.1 19.7 %custom-call.14 = f32[2,128,128]{1,2,0:T(8,128)S(1)} custom-call(f32[2,128,128]{2,1,0:T(8,128)S(1)} %get-tuple-element.21), custom_call_target="InvertDiagBlocksLowerTriangular" | custom-call | tf_op jit(solution)/shard_map/triangular_solve/custom-call.0 | solution.py:36
  429.8 0.3 fusion.15
  430.1 0.2 fusion.13
  430.3 0.3 fusion.12
  430.6 1.1 fusion.3
  431.7 0.0 all-reduce.6.cloned.1.call-update
  431.7 0.2 all-gather.2.cloned.1.call-start
  431.9 140.5 %all-reduce.6.cloned.1.call-done = f32[256,256]{0,1:T(8,128)} async-done(((f32[256,256]{0,1:T(8,128)}), f32[256,256]{0,1:T(8,128)}) %all-reduce.6.cloned.1.call-update) | async-done | bytes 262160 | tf_op jit(solution)/shard_map/psum | solution.py:40
  572.4 1.1 copy.7
  573.5 1.0 fusion.1
  574.5 11.7 %cholesky.164 = f32[128,128]{1,0:T(8,128)S(1)} custom-call(f32[128,128]{1,0:T(8,128)S(1)} %cholesky.197), custom_call_target="Cholesky" | custom-call | tf_op jit(solution)/shard_map/jit(cholesky)/cholesky | solution.py:35
  586.3 9.8 %custom-call.15 = f32[1,128,128]{1,2,0:T(8,128)S(1)} custom-call(f32[1,128,128]{2,1,0:T(8,128)S(1)} %get-tuple-element.46), custom_call_target="InvertDiagBlocksLowerTriangular" | custom-call | tf_op jit(solution)/shard_map/jit(cholesky)/cholesky | solution.py:35
  596.1 0.2 constant_dynamic-update-slice_fusion.1
  596.3 0.3 convolution_subtract_fusion.1
  596.6 11.7 %cholesky.181 = f32[128,128]{1,0:T(8,128)S(1)} custom-call(f32[128,128]{1,0:T(8,128)S(1)} %convolution_subtract_fusion.1), custom_call_target="Cholesky" | custom-call | tf_op jit(solution)/shard_map/jit(cholesky)/cholesky | solution.py:35
  608.3 0.6 compare_reduce_fusion.1
  609.0 0.7 compare_reduce_fusion
  611.1 4.3 while.5
  611.3 0.6 fusion.46
  611.9 1.4 bitcast_dynamic-update-slice_fusion.5
  613.4 0.6 fusion.46
  614.0 1.4 bitcast_dynamic-update-slice_fusion.5
  615.4 19.7 %custom-call.16 = f32[2,128,128]{1,2,0:T(8,128)S(1)} custom-call(f32[2,128,128]{2,1,0:T(8,128)S(1)} %get-tuple-element.22), custom_call_target="InvertDiagBlocksLowerTriangular" | custom-call | tf_op jit(solution)/shard_map/triangular_solve/custom-call.0 | solution.py:36
  635.1 0.3 fusion.9
  635.4 0.2 convolution_subtract_fusion
  635.6 0.3 fusion.7
  635.9 0.7 maximum_multiply_fusion
  636.6 0.0 all-gather.2.cloned.1.call-update
  636.6 46.4 %all-gather.2.cloned.1.call-done = f32[4096,256]{0,1:T(8,128)} async-done(((f32[128,256]{0,1:T(8,128)}), f32[4096,256]{0,1:T(8,128)}) %all-gather.2.cloned.1.call-update) | async-done | bytes 4194320 | tf_op jit(solution)/shard_map/all_gather | solution.py:65
  683.0 5.6 copy.8
  (17 shorter events, 0.3 us)
Async XLA Ops:
  6.5 212.3 %reduce-scatter.2.cloned.1.call-start = ((), (), s32[]{:S(2)}) async-start(), calls=%async_computation.1 | async-start | bytes 4325376 | tf_op jit(solution)/shard_map/reduce_scatter | solution.py:49
  6.5 113.4 %copy-start = (bf16[2048,4096]{1,0:T(8,128)(2,1)S(1)}, bf16[2048,4096]{1,0:T(8,128)(2,1)}, u32[]{:S(2)}) copy-start(bf16[2048,4096]{1,0:T(8,128)(2,1)} %param.5) | copy-start | bytes 50331652
  24.1 47.9 %collective-permute-start = (f32[2048,256]{1,0:T(8,128)S(1)}, f32[2048,256]{1,0:T(8,128)S(1)}, u32[]{:S(2)}, u32[]{:S(2)}) collective-permute-start(f32[2048,256]{1,0:T(8,128)S(1)} %fusion.29), channel_id=1, source_target_pairs={{0,32},{32,0},{64,96},{96,64},{1,33},{33,1},{65,97},{97,65},{2,34}... | collective-permute-start | bytes 6291464 | tf_op jit(solution)/shard_map/ppermute | solution.py:17
  72.2 47.7 %collective-permute-start.1 = (f32[2048,256]{1,0:T(8,128)S(1)}, f32[2048,256]{1,0:T(8,128)S(1)}, u32[]{:S(2)}, u32[]{:S(2)}) collective-permute-start(f32[2048,256]{1,0:T(8,128)S(1)} %add.35), channel_id=1, source_target_pairs={{0,64},{32,96},{64,0},{96,32},{1,65},{33,97},{65,1},{97,33},{2,66}... | collective-permute-start | bytes 6291464 | tf_op jit(solution)/shard_map/ppermute | solution.py:17
  134.9 233.0 %all-reduce.4.cloned.1.call-start = ((), (), s32[]{:S(2)}) async-start(), calls=%async_computation.2 | async-start | bytes 524288 | tf_op jit(solution)/shard_map/psum | solution.py:40
  220.9 351.6 %all-reduce.6.cloned.1.call-start = ((), (), s32[]{:S(2)}) async-start(), calls=%async_computation.3 | async-start | bytes 524288 | tf_op jit(solution)/shard_map/psum | solution.py:40
  431.7 251.3 %all-gather.2.cloned.1.call-start = ((), (), s32[]{:S(2)}) async-start(), calls=%async_computation.4 | async-start | bytes 4325376 | tf_op jit(solution)/shard_map/all_gather | solution.py:65
Sparse Core Ops, SparseCore 0:
  135.1 83.7 reduce-scatter.1
  223.6 144.2 all-reduce.3
  431.8 140.5 all-reduce.5
  636.7 46.2 all-gather.1
